TPU v7x, 32 devices: a whole 2x2x4 slice. The times are simulated.
32 devices in a mesh: vec: 4 (over y, x), orb: 8 (over z, core).
Axes of the slice: x: 2, y: 2, z: 4, core: 2. Of those that a mesh axis runs over, the one named last changes fastest.
Arguments:
- chol_occ: float32 [44, 96, 1056], P('vec', 'orb'), may hold values from -6 to 6
- chol_vir: float32 [44, 960, 1056], P('vec', 'orb'), may hold values from -6 to 6
- singles: float32 [96, 960], P('orb'), may hold values from -0.6 to 0.6
Outputs:
- dressed_vir: float32 [44, 960, 1056], P('vec', 'orb')
- dressed_ov: float32 [44, 96, 960], P(None, 'orb', 'vec')
- fock_ov: float32 [96, 960], P('orb')
All inputs are finite; a program needn't handle non-finite values.
Results may differ from a plain program's by a relative error of at most 0.000086.
Values sent between devices are 32-bit elements; how exact they have to be, the bound alone decides.
A program may use at most 64 MiB of HBM per device.

v0:
```python
import jax
import jax.numpy as jnp
from jax import lax
from jax.sharding import PartitionSpec as P


def dress_right(matrix_rows, amplitudes):
    occ_width = amplitudes.shape[0]
    occ_cols = matrix_rows[:, :, :occ_width]
    extra_term = jnp.einsum("qrj,ja->qra", occ_cols, amplitudes, precision=lax.Precision.HIGHEST)
    return jnp.concatenate([occ_cols, matrix_rows[:, :, occ_width:] + extra_term], axis=2)


def dress_left(vir_rows, occ_all, amp_cols):
    return vir_rows - jnp.einsum("qin,ia->qan", occ_all, amp_cols, precision=lax.Precision.HIGHEST)


def shards(chol_occ, chol_vir, singles):
    amplitudes = lax.all_gather(singles, "orb", axis=0, tiled=True)
    occ_width = amplitudes.shape[0]
    vir_local = chol_vir.shape[1]
    vir_start = lax.axis_index("orb") * vir_local
    amp_cols = lax.dynamic_slice_in_dim(amplitudes, vir_start, vir_local, 1)
    occ_all = lax.all_gather(chol_occ, "orb", axis=1, tiled=True)
    dressed_vir = dress_right(dress_left(chol_vir, occ_all, amp_cols), amplitudes)
    dressed_occ = dress_right(chol_occ, amplitudes)
    local_rows = chol_occ.shape[1]
    first_row = lax.axis_index("orb") * local_rows
    row_ids = lax.broadcasted_iota(jnp.int32, (local_rows, chol_occ.shape[2]), 0) + first_row
    col_ids = lax.broadcasted_iota(jnp.int32, (local_rows, chol_occ.shape[2]), 1)
    diag_mask = jnp.where(row_ids == col_ids, 1.0, 0.0).astype(jnp.float32)
    traces_local = jnp.sum(chol_occ * diag_mask[None], axis=(1, 2))
    traces = lax.psum(traces_local, "orb")
    ov_block = dressed_occ[:, :, occ_width:]
    total_vectors = chol_occ.shape[0] * lax.axis_size("vec")
    fock_part = (
        jnp.einsum("q,qia->ia", traces, ov_block, precision=lax.Precision.HIGHEST) / total_vectors
    )
    fock_ov = lax.psum(fock_part, "vec")
    pair_blocks = lax.all_to_all(ov_block, "vec", split_axis=2, concat_axis=0, tiled=True)
    return (dressed_vir, pair_blocks, fock_ov)


def solution(mesh):
    return jax.shard_map(
        shards,
        mesh=mesh,
        in_specs=(P("vec", "orb", None), P("vec", "orb", None), P("orb", None)),
        out_specs=(P("vec", "orb", None), P(None, "orb", "vec"), P("orb", None)),
        check_vma=False,
    )
```

profile of v0, /device:TPU:0, one launch (start us, length us, event | category | flops | bytes accessed | tf_op | source)
XLA Modules:
  0.0 127.6 jit_solution(5254257879419233849)
XLA Ops:
  7.2 0.0 all-gather.3.cloned.1.call-start
  7.2 2.3 %copy.10 = f32[11,12,1056]{2,0,1:T(8,128)} copy(f32[11,12,1056]{2,1,0:T(8,128)} %param.3) | data formatting | bytes 1115136 | tf_op args[0]
  9.5 0.0 all-gather.3.cloned.1.call-update
  9.5 16.7 %all-gather = f32[8,12,960]{2,1,0:T(8,128)S(1)} all-gather(f32[1,12,960]{2,1,0:T(8,128)} %bitcast.22), channel_id=1, replica_groups=mesh['vec'=4,'orb'=8] {'orb'}, dimensions={0}, use_global_device_ids=true | all-gather | bytes 414720 | tf_op jit(solution)/shard_map/all_gather | solution.py:19
  26.3 1.9 %convolution_add_fusion = f32[11,12,960]{2,1,0:T(8,128)S(1)} fusion(f32[96,960,1]{1,0,2:T(8,128)S(1)} %reshape.23, f32[11,12,1056]{2,1,0:T(8,128)} %param.3), kind=kOutput, calls=%fused_computation.4 | convolution fusion | flops 146108160 | bytes 1433088 | tf_op jit(solution)/shard_map/qrj,ja->qra/dot_general | solution.py:10
  28.2 6.0 %copy.13 = f32[11,12,960]{1,0,2:T(8,128)} copy(f32[11,12,960]{2,1,0:T(8,128)S(1)} %convolution_add_fusion) | data formatting | bytes 1013760 | tf_op jit(solution)/shard_map/add | solution.py:11
  34.2 0.0 copy-start
  34.2 6.5 %reshape.27 = f32[4,1,31680]{2,1,0:T(1,128)} reshape(f32[960,11,12]{2,1,0:T(8,128)} %bitcast.20) | data formatting | bytes 1013760
  40.7 0.1 fusion.4
  40.8 0.0 copy-done
  40.8 0.2 multiply_reduce_fusion
  41.0 3.7 %all-to-all-start = ((f32[4,1,31680]{2,1,0:T(1,128)}), f32[4,1,31680]{2,1,0:T(1,128)S(1)}, u32[]{:S(2)}, u32[]{:S(2)}) async-start(f32[4,1,31680]{2,1,0:T(1,128)} %reshape.27), calls=%async_computation | async-start | bytes 1015808 | tf_op jit(solution)/shard_map/all_to_all | solution.py:40
  44.7 19.3 %psum.14 = f32[11]{0:T(128)S(1)} all-reduce(f32[11]{0:T(128)S(1)} %multiply_reduce_fusion), channel_id=1, replica_groups=mesh['vec'=4,'orb'=8] {'orb'}, use_global_device_ids=true, to_apply=%region_1.2 | all-reduce | flops 11 | bytes 88 | tf_op jit(solution)/shard_map/psum | solution.py:33
  64.0 0.8 fusion.1
  64.9 17.7 %psum.15 = f32[12,960]{1,0:T(8,128)} all-reduce(f32[12,960]{1,0:T(8,128)S(1)} %bitcast_multiply_fusion), channel_id=1, replica_groups=mesh['vec'=4,'orb'=8] {'vec'}, use_global_device_ids=true, to_apply=%region_2.3 | all-reduce | flops 11520 | bytes 92160 | tf_op jit(solution)/shard_map/psum | solution.py:39
  82.5 0.0 all-to-all-done
  82.5 0.5 broadcast.18
  83.0 2.1 %reduce = f32[4,31680]{1,0:T(4,128)S(1)} reduce(f32[4,1,31680]{2,1,0:T(1,128)S(1)} %all-to-all-done, f32[]{:T(128)} %broadcast.18), dimensions={1}, to_apply=%all_to_all.13.reduce_sub_computation | reduce | bytes 1013764 | tf_op jit(solution)/shard_map/all_to_all | solution.py:40
  85.2 6.0 %reshape.28 = f32[960,11,12]{2,1,0:T(8,128)} reshape(f32[4,31680]{1,0:T(4,128)S(1)} %reduce) | data formatting | bytes 1013760
  91.2 6.2 %copy.14 = f32[11,12,4,240]{3,0,2,1:T(8,128)S(1)} copy(f32[11,12,4,240]{1,0,3,2:T(8,128)} %bitcast.19) | data formatting | bytes 1013760 | tf_op jit(solution)/shard_map/all_to_all | solution.py:40
  97.4 0.9 all_to_all.16
  98.3 14.5 %bitcast_subtract_fusion = f32[11,120,1056]{1,2,0:T(8,128)S(1)} fusion(f32[11,120,1056]{1,2,0:T(8,128)} %param.4, f32[11,96,1056]{2,0,1:T(8,128)} %all-gather.3.cloned.1.call-done, f32[96,960]{1,0:T(8,128)S(1)} %reshape.21, s32[]{:T(128)S(6)} %select_n.11), kind=kOutput, calls=%fused_computation.1 | convolution fusion | flops 1607189760 | bytes 15661060 | tf_op jit(solution)/shard_map/qin,ia->qan/dot_general | solution.py:15
  112.9 4.7 %slice_add_fusion = f32[11,120,960]{1,2,0:T(8,128)S(1)} fusion(f32[11,120,1056]{1,2,0:T(8,128)S(1)} %bitcast_subtract_fusion, f32[96,960,1]{1,0,2:T(8,128)S(1)} %reshape.23), kind=kOutput, calls=%fused_computation.2 | convolution fusion | flops 1461081600 | bytes 11013120 | tf_op jit(solution)/shard_map/qrj,ja->qra/dot_general | solution.py:10
  117.6 3.2 %pad_maximum_fusion = f32[11,120,1056]{1,2,0:T(8,128)} fusion(f32[11,120,960]{1,2,0:T(8,128)S(1)} %slice_add_fusion, f32[11,120,96]{1,2,0:T(8,128)S(1)} %slice.16), kind=kLoop, calls=%fused_computation | loop fusion | flops 1393920 | bytes 11151360 | tf_op jit(solution)/shard_map/concatenate | solution.py:11
  (6 shorter events, 0.1 us)
Async XLA Ops:
  7.2 91.1 %all-gather.3.cloned.1.call-start = ((), (), s32[]{:S(2)}) async-start(), calls=%async_computation.1 | async-start | bytes 7962624 | tf_op jit(solution)/shard_map/all_gather | solution.py:24
  34.2 6.6 %copy-start = (f32[11,12,1056]{2,1,0:T(8,128)S(1)}, f32[11,12,1056]{2,1,0:T(8,128)}, u32[]{:S(2)}) copy-start(f32[11,12,1056]{2,1,0:T(8,128)} %param.3) | copy-start | bytes 1672708
  41.0 41.6 %all-to-all-start = ((f32[4,1,31680]{2,1,0:T(1,128)}), f32[4,1,31680]{2,1,0:T(1,128)S(1)}, u32[]{:S(2)}, u32[]{:S(2)}) async-start(f32[4,1,31680]{2,1,0:T(1,128)} %reshape.27), calls=%async_computation | async-start | bytes 1015808 | tf_op jit(solution)/shard_map/all_to_all | solution.py:40
Sparse Core Ops, SparseCore 0:
  10.2 74.4 all-gather.2
where the time goes:
time: 128 us
  blocking collectives  53.7 us (42%)
  local copies, waits for them, and re-layouts  28.5 us (22%)
  matrix products  22 us (17%)
  between operations  14.1 us (11%)
  other arithmetic  5.58 us (4%)
  starting transfers between devices  3.76 us (3%)
    psum x1, blocking collectives, shards(): traces = lax.psum(traces_local, 'orb')  19.3 us
    psum x1, blocking collectives, shards(): fock_ov = lax.psum(fock_part, 'vec')  17.7 us
    all_gather x1, blocking collectives, shards(): amplitudes = lax.all_gather(singles, 'orb', axis=0, tiled=True)  16.7 us
    unnamed x7, local copies, waits for them, and re-layouts  14.9 us
    dot_general x1, matrix products, dress_left(): jnp.einsum('qin,ia->qan', occ_all, amp_cols, precision=lax.Precision.HIGH...  14.5 us
    all_to_all x3, local copies, waits for them, and re-layouts, shards(): lax.all_to_all(ov_block, 'vec', split_axis=2, concat_axis=0, tiled=True)  7.57 us
    dot_general x2, matrix products, dress_right(): jnp.einsum('qrj,ja->qra', occ_cols, amplitudes, precision=lax.Precision.H...  6.66 us
    add x1, local copies, waits for them, and re-layouts, dress_right(): matrix_rows[:, :, occ_width:] + extra_term  5.96 us
  transfers between devices with their start and end apart: 2, of which 0 were waited for; matrix products, arithmetic and copies ran while one was open for 24% of the time, Pallas kernels for 0%

commit v1 on v0

--- a/solution.py
+++ b/solution.py
@@ -2,6 +2,15 @@
 import jax.numpy as jnp
 from jax import lax
 from jax.sharding import PartitionSpec as P
+
+
+def doubling_sum(shard, axis):
+    size = lax.axis_size(axis)
+    acc, far = (shard, 1)
+    while far < size:
+        acc = acc + lax.ppermute(acc, axis, [(i, i ^ far) for i in range(size)])
+        far = 2 * far
+    return acc
 
 
 def dress_right(matrix_rows, amplitudes):
@@ -36,7 +45,7 @@
     fock_part = (
         jnp.einsum("q,qia->ia", traces, ov_block, precision=lax.Precision.HIGHEST) / total_vectors
     )
-    fock_ov = lax.psum(fock_part, "vec")
+    fock_ov = doubling_sum(fock_part, "vec")
     pair_blocks = lax.all_to_all(ov_block, "vec", split_axis=2, concat_axis=0, tiled=True)
     return (dressed_vir, pair_blocks, fock_ov)
 

time: 128 us -> 120 us (0.938)
  blocking collectives: 53.7 us -> 36.2 us
  waiting for transfers between devices: 0.02 us -> 5.16 us
  starting transfers between devices: 3.76 us -> 7.24 us
    psum x1 -> x0, blocking collectives: 17.7 us -> none  [shards(): fock_ov = lax.psum(fock_part, 'vec')]
    ppermute x0 -> x2, waiting for transfers between devices: none -> 5.14 us  [doubling_sum(): acc = acc + lax.ppermute(acc, axis, [(i, i ^ far) for i in range(size)])]
    ppermute x0 -> x2, starting transfers between devices: none -> 3.48 us  [doubling_sum(): acc = acc + lax.ppermute(acc, axis, [(i, i ^ far) for i in range(size)])]
  transfers between devices with their start and end apart: 2 -> 4, of which waited for: 0 -> 2; matrix products, arithmetic and copies ran while one was open for 24% -> 26% of each run, Pallas kernels for 0% -> 0%
where the time goes in v1:
time: 120 us; the launch traced here: 119 us
  blocking collectives  36.2 us (30%)
  local copies, waits for them, and re-layouts  28.5 us (24%)
  matrix products  22 us (18%)
  between operations  14.1 us (12%)
  starting transfers between devices  7.24 us (6%)
  other arithmetic  6.23 us (5%)
  waiting for transfers between devices  5.16 us (4%)
    psum x1, blocking collectives, shards(): traces = lax.psum(traces_local, 'orb')  19.5 us
    all_gather x1, blocking collectives, shards(): amplitudes = lax.all_gather(singles, 'orb', axis=0, tiled=True)  16.7 us
    unnamed x7, local copies, waits for them, and re-layouts  14.9 us
    dot_general x1, matrix products, dress_left(): jnp.einsum('qin,ia->qan', occ_all, amp_cols, precision=lax.Precision.HIGH...  14.5 us
    all_to_all x3, local copies, waits for them, and re-layouts, shards(): lax.all_to_all(ov_block, 'vec', split_axis=2, concat_axis=0, tiled=True)  7.6 us
    dot_general x2, matrix products, dress_right(): jnp.einsum('qrj,ja->qra', occ_cols, amplitudes, precision=lax.Precision.H...  6.66 us
    add x1, local copies, waits for them, and re-layouts, dress_right(): matrix_rows[:, :, occ_width:] + extra_term  5.96 us
    ppermute x2, waiting for transfers between devices, doubling_sum(): acc = acc + lax.ppermute(acc, axis, [(i, i ^ far) for i in range(size)])  5.14 us
  transfers between devices with their start and end apart: 4, of which 2 were waited for; matrix products, arithmetic and copies ran while one was open for 26% of the time, Pallas kernels for 0%

profile of v1, /device:TPU:0, one launch (start us, length us, event | category | flops | bytes accessed | tf_op | source)
XLA Modules:
  0.0 119.5 jit_solution(11190042272631445356)
XLA Ops:
  7.2 0.0 all-gather.3.cloned.1.call-start
  7.2 2.3 %copy.10 = f32[11,12,1056]{2,0,1:T(8,128)} copy(f32[11,12,1056]{2,1,0:T(8,128)} %param.3) | data formatting | bytes 1115136 | tf_op args[0]
  9.5 16.7 %all-gather = f32[8,12,960]{2,1,0:T(8,128)S(1)} all-gather(f32[1,12,960]{2,1,0:T(8,128)} %bitcast.24), channel_id=1, replica_groups=mesh['vec'=4,'orb'=8] {'orb'}, dimensions={0}, use_global_device_ids=true | all-gather | bytes 414720 | tf_op jit(solution)/shard_map/all_gather | solution.py:28
  26.3 1.9 %convolution_add_fusion = f32[11,12,960]{2,1,0:T(8,128)S(1)} fusion(f32[96,960,1]{1,0,2:T(8,128)S(1)} %reshape.23, f32[11,12,1056]{2,1,0:T(8,128)} %param.3), kind=kOutput, calls=%fused_computation.4 | convolution fusion | flops 146108160 | bytes 1433088 | tf_op jit(solution)/shard_map/qrj,ja->qra/dot_general | solution.py:19
  28.2 6.0 %copy.13 = f32[11,12,960]{1,0,2:T(8,128)} copy(f32[11,12,960]{2,1,0:T(8,128)S(1)} %convolution_add_fusion) | data formatting | bytes 1013760 | tf_op jit(solution)/shard_map/add | solution.py:20
  34.2 6.5 %reshape.27 = f32[4,1,31680]{2,1,0:T(1,128)} reshape(f32[960,11,12]{2,1,0:T(8,128)} %bitcast.22) | data formatting | bytes 1013760
  40.7 0.1 fusion.4
  40.8 0.2 multiply_reduce_fusion
  41.0 3.7 %all-to-all-start = ((f32[4,1,31680]{2,1,0:T(1,128)}), f32[4,1,31680]{2,1,0:T(1,128)S(1)}, u32[]{:S(2)}, u32[]{:S(2)}) async-start(f32[4,1,31680]{2,1,0:T(1,128)} %reshape.27), calls=%async_computation | async-start | bytes 1015808 | tf_op jit(solution)/shard_map/all_to_all | solution.py:49
  44.7 19.5 %psum.7 = f32[11]{0:T(128)S(1)} all-reduce(f32[11]{0:T(128)S(1)} %multiply_reduce_fusion), channel_id=1, replica_groups=mesh['vec'=4,'orb'=8] {'orb'}, use_global_device_ids=true, to_apply=%region_1.2 | all-reduce | flops 11 | bytes 88 | tf_op jit(solution)/shard_map/psum | solution.py:42
  64.2 0.8 fusion.1
  65.0 1.7 %collective-permute-start = (f32[12,960]{1,0:T(8,128)S(1)}, f32[12,960]{1,0:T(8,128)S(1)}, u32[]{:S(2)}, u32[]{:S(2)}) collective-permute-start(f32[12,960]{1,0:T(8,128)S(1)} %bitcast_multiply_fusion), channel_id=1, source_target_pairs={{0,8},{8,0},{16,24},{24,16},{1,9},{9,1},{17,25},{25,17},{2,10},{10... | collective-permute-start | bytes 138248 | tf_op jit(solution)/shard_map/ppermute | solution.py:11
  66.8 2.6 %collective-permute-done = f32[12,960]{1,0:T(8,128)S(1)} collective-permute-done((f32[12,960]{1,0:T(8,128)S(1)}, f32[12,960]{1,0:T(8,128)S(1)}, u32[]{:S(2)}, u32[]{:S(2)}) %collective-permute-start) | collective-permute-done | bytes 46112 | tf_op jit(solution)/shard_map/ppermute | solution.py:11
  69.4 1.7 %collective-permute-start.1 = (f32[12,960]{1,0:T(8,128)S(1)}, f32[12,960]{1,0:T(8,128)S(1)}, u32[]{:S(2)}, u32[]{:S(2)}) collective-permute-start(f32[12,960]{1,0:T(8,128)S(1)} %fusion.8), channel_id=1, source_target_pairs={{0,16},{8,24},{16,0},{24,8},{1,17},{9,25},{17,1},{25,9},{2,18},{10... | collective-permute-start | bytes 138248 | tf_op jit(solution)/shard_map/ppermute | solution.py:11
  71.2 2.5 %collective-permute-done.1 = f32[12,960]{1,0:T(8,128)S(1)} collective-permute-done((f32[12,960]{1,0:T(8,128)S(1)}, f32[12,960]{1,0:T(8,128)S(1)}, u32[]{:S(2)}, u32[]{:S(2)}) %collective-permute-start.1) | collective-permute-done | bytes 46112 | tf_op jit(solution)/shard_map/ppermute | solution.py:11
  73.7 0.6 add.30
  74.3 0.5 broadcast.18
  74.9 2.1 %reduce = f32[4,31680]{1,0:T(4,128)S(1)} reduce(f32[4,1,31680]{2,1,0:T(1,128)S(1)} %all-to-all-done, f32[]{:T(128)} %broadcast.18), dimensions={1}, to_apply=%all_to_all.13.reduce_sub_computation | reduce | bytes 1013764 | tf_op jit(solution)/shard_map/all_to_all | solution.py:49
  77.0 6.0 %reshape.28 = f32[960,11,12]{2,1,0:T(8,128)} reshape(f32[4,31680]{1,0:T(4,128)S(1)} %reduce) | data formatting | bytes 1013760
  83.0 6.2 %copy.14 = f32[11,12,4,240]{3,0,2,1:T(8,128)S(1)} copy(f32[11,12,4,240]{1,0,3,2:T(8,128)} %bitcast.21) | data formatting | bytes 1013760 | tf_op jit(solution)/shard_map/all_to_all | solution.py:49
  89.2 0.9 all_to_all.16
  90.1 14.5 %bitcast_subtract_fusion = f32[11,120,1056]{1,2,0:T(8,128)S(1)} fusion(f32[11,120,1056]{1,2,0:T(8,128)} %param.4, f32[11,96,1056]{2,0,1:T(8,128)} %all-gather.3.cloned.1.call-done, f32[96,960]{1,0:T(8,128)S(1)} %reshape.21, s32[]{:T(128)S(6)} %select_n.11), kind=kOutput, calls=%fused_computation.1 | convolution fusion | flops 1607189760 | bytes 15661060 | tf_op jit(solution)/shard_map/qin,ia->qan/dot_general | solution.py:24
  104.7 4.7 %slice_add_fusion = f32[11,120,960]{1,2,0:T(8,128)S(1)} fusion(f32[11,120,1056]{1,2,0:T(8,128)S(1)} %bitcast_subtract_fusion, f32[96,960,1]{1,0,2:T(8,128)S(1)} %reshape.23), kind=kOutput, calls=%fused_computation.2 | convolution fusion | flops 1461081600 | bytes 11013120 | tf_op jit(solution)/shard_map/qrj,ja->qra/dot_general | solution.py:19
  109.5 3.2 %pad_maximum_fusion = f32[11,120,1056]{1,2,0:T(8,128)} fusion(f32[11,120,960]{1,2,0:T(8,128)S(1)} %slice_add_fusion, f32[11,120,96]{1,2,0:T(8,128)S(1)} %slice.16), kind=kLoop, calls=%fused_computation | loop fusion | flops 1393920 | bytes 11151360 | tf_op jit(solution)/shard_map/concatenate | solution.py:20
  (11 shorter events, 0.2 us)
Async XLA Ops:
  7.2 83.0 %all-gather.3.cloned.1.call-start = ((), (), s32[]{:S(2)}) async-start(), calls=%async_computation.1 | async-start | bytes 7962624 | tf_op jit(solution)/shard_map/all_gather | solution.py:33
  34.2 6.6 %copy-start = (f32[11,12,1056]{2,1,0:T(8,128)S(1)}, f32[11,12,1056]{2,1,0:T(8,128)}, u32[]{:S(2)}) copy-start(f32[11,12,1056]{2,1,0:T(8,128)} %param.3) | copy-start | bytes 1672708
  41.0 33.4 %all-to-all-start = ((f32[4,1,31680]{2,1,0:T(1,128)}), f32[4,1,31680]{2,1,0:T(1,128)S(1)}, u32[]{:S(2)}, u32[]{:S(2)}) async-start(f32[4,1,31680]{2,1,0:T(1,128)} %reshape.27), calls=%async_computation | async-start | bytes 1015808 | tf_op jit(solution)/shard_map/all_to_all | solution.py:49
  65.0 4.3 %collective-permute-start = (f32[12,960]{1,0:T(8,128)S(1)}, f32[12,960]{1,0:T(8,128)S(1)}, u32[]{:S(2)}, u32[]{:S(2)}) collective-permute-start(f32[12,960]{1,0:T(8,128)S(1)} %bitcast_multiply_fusion), channel_id=1, source_target_pairs={{0,8},{8,0},{16,24},{24,16},{1,9},{9,1},{17,25},{25,17},{2,10},{10... | collective-permute-start | bytes 138248 | tf_op jit(solution)/shard_map/ppermute | solution.py:11
  69.4 4.3 %collective-permute-start.1 = (f32[12,960]{1,0:T(8,128)S(1)}, f32[12,960]{1,0:T(8,128)S(1)}, u32[]{:S(2)}, u32[]{:S(2)}) collective-permute-start(f32[12,960]{1,0:T(8,128)S(1)} %fusion.8), channel_id=1, source_target_pairs={{0,16},{8,24},{16,0},{24,8},{1,17},{9,25},{17,1},{25,9},{2,18},{10... | collective-permute-start | bytes 138248 | tf_op jit(solution)/shard_map/ppermute | solution.py:11
Sparse Core Ops, SparseCore 0:
  10.2 74.4 all-gather.2
